TPU v7x, 256 devices: a whole 4x4x8 slice. The times are simulated.
256 devices in a mesh: seq: 16 (over x_hi, z), rep: 16 (over y, x_lo, core).
Axes of the slice: x: 4 (x_hi: 2, x_lo: 2; x = x_hi * 2 + x_lo), y: 4, z: 8, core: 2. Of those that a mesh axis runs over, the one named last changes fastest.
Arguments:
- t_query: bfloat16 [16, 2048, 4096], P('rep', 'seq'), may hold values from -45 to 45
- t_key: bfloat16 [16, 2048, 512], P('rep', 'seq'), may hold values from -4 to 4
- t_value: bfloat16 [16, 2048, 512], P('rep', 'seq'), may hold values from -6 to 6
- s_query: bfloat16 [16, 2048, 2048], P('rep', 'seq'), may hold values from -45 to 45
- s_key: bfloat16 [16, 2048, 512], P('rep', 'seq'), may hold values from -4 to 4
- student_value: bfloat16 [16, 2048, 512], P('rep', 'seq'), may hold values from -6 to 6
- student_wo: bfloat16 [2048, 2048], P('seq'), may hold values from -0.125 to 0.125
- projection: bfloat16 [4096, 2048], P('seq'), may hold values from -0.09375 to 0.09375
- doc_ids: int32 [16, 2048], P('rep'), may hold values from 0 to 15, never falling along the last dimension, each value on 1 to 512 neighbouring positions
- span_order: int32 [16, 32], P('rep'), may hold values from 0 to 31, each once within a row
Outputs:
- seq_loss: float32 [16], P('rep')
- d_wo: float32 [2048, 2048], P('seq', 'rep')
- d_query: bfloat16 [16, 2048, 2048], P('rep', 'seq')
- d_key: bfloat16 [16, 2048, 512], P('rep', 'seq')
- d_value: bfloat16 [16, 2048, 512], P('rep', 'seq')
All inputs are finite; a program needn't handle non-finite values.
Results may differ from a plain program's by a relative error of at most 0.018.
The roundings to bfloat16 on the way count: a program that leaves them out, or rounds other values in their place, can miss the bound.
Values may be sent and summed in bfloat16 or wider, within the bound.
No kernel may reach another device: no remote copies, remote signals or barrier semaphores. Data moves between devices by JAX's collectives and lax.ppermute only.
A program may use at most 128 MiB of HBM per device.

v0:
```python
import math
import jax
import jax.numpy as jnp
from jax import lax
from jax.sharding import PartitionSpec as P

HEAD_WIDTH = 128
MASKED = -1e30


def stored_positions(order_row, length):
    half_len = length // order_row.shape[0]
    offsets = jnp.arange(half_len, dtype=jnp.int32)
    return (order_row[:, None] * half_len + offsets[None, :]).reshape(length)


def head_attention(queries, key_rows, val_rows, positions, stored_docs):
    length = queries.shape[0]
    row_block = math.gcd(length, 512)
    scaling = 1.0 / math.sqrt(HEAD_WIDTH)

    def one_block(block_id):
        first_row = block_id * row_block
        q_block = lax.dynamic_slice_in_dim(queries, first_row, row_block, 0)
        q_pos = lax.dynamic_slice_in_dim(positions, first_row, row_block, 0)
        q_docs = lax.dynamic_slice_in_dim(stored_docs, first_row, row_block, 0)
        allowed = (q_docs[:, None] == stored_docs[None, :]) & (positions[None, :] <= q_pos[:, None])
        scores = (
            jnp.einsum("qhd,kd->hqk", q_block, key_rows, preferred_element_type=jnp.float32)
            * scaling
        )
        scores = jnp.where(allowed, scores, MASKED)
        maximum = jnp.max(scores, axis=2, keepdims=True)
        weights = jnp.where(allowed, jnp.exp(scores - maximum), 0.0)
        totals = jnp.sum(weights, axis=2, keepdims=True)
        prob_rows = (weights / totals).astype(jnp.bfloat16)
        mixed_rows = jnp.einsum(
            "hqk,kd->qhd", prob_rows, val_rows, preferred_element_type=jnp.float32
        )
        return (prob_rows, mixed_rows.astype(jnp.bfloat16))

    block_ids = jnp.arange(length // row_block, dtype=jnp.int32)
    return lax.map(one_block, block_ids)


def shards(
    t_query,
    t_key,
    t_value,
    s_query,
    s_key,
    student_value,
    student_wo,
    projection,
    doc_ids,
    span_order,
):
    groups = lax.axis_size("seq")
    my_index = lax.axis_index("seq")
    tokens = t_query.shape[1]
    length = tokens * groups
    scaling = 1.0 / math.sqrt(HEAD_WIDTH)
    positions = stored_positions(span_order[0], length)
    stored_docs = jnp.take(doc_ids[0], positions)
    first_own = my_index * tokens
    own_pos = lax.dynamic_slice_in_dim(positions, first_own, tokens, 0)
    own_docs = lax.dynamic_slice_in_dim(stored_docs, first_own, tokens, 0)
    t_heads_all = t_query.shape[2] // HEAD_WIDTH
    t_kv = t_key.shape[2] // HEAD_WIDTH
    t_local = t_heads_all // groups
    t_share = t_heads_all // t_kv
    own_queries = t_query[0].reshape(tokens, t_kv, t_share, HEAD_WIDTH)
    start_state = (
        jnp.full((t_kv, t_share, tokens), MASKED, jnp.float32),
        jnp.zeros((t_kv, t_share, tokens), jnp.float32),
        jnp.zeros((t_kv, t_share, tokens, HEAD_WIDTH), jnp.float32),
    )
    carried = start_state
    key_piece = lax.all_gather(t_key[0], "seq", axis=0, tiled=True)
    val_piece = lax.all_gather(t_value[0], "seq", axis=0, tiled=True)
    row_count = key_piece.shape[0]
    sub_rows = math.gcd(row_count, 512)
    for offset in range(0, row_count, sub_rows):
        key_block = key_piece[offset : offset + sub_rows].reshape(sub_rows, t_kv, HEAD_WIDTH)
        val_block = val_piece[offset : offset + sub_rows].reshape(sub_rows, t_kv, HEAD_WIDTH)
        key_pos = lax.dynamic_slice_in_dim(positions, offset, sub_rows, 0)
        key_docs = lax.dynamic_slice_in_dim(stored_docs, offset, sub_rows, 0)
        allowed = (own_docs[:, None] == key_docs[None, :]) & (key_pos[None, :] <= own_pos[:, None])

        def absorb(states):
            running_max, running_sum, accumulated = states
            scores = (
                jnp.einsum(
                    "tkgd,skd->kgts", own_queries, key_block, preferred_element_type=jnp.float32
                )
                * scaling
            )
            scores = jnp.where(allowed, scores, MASKED)
            new_max = jnp.maximum(running_max, jnp.max(scores, axis=3))
            weights = jnp.where(allowed, jnp.exp(scores - new_max[..., None]), 0.0)
            factor = jnp.exp(running_max - new_max)
            running_sum = running_sum * factor + jnp.sum(weights, axis=3)
            accumulated = accumulated * factor[..., None] + jnp.einsum(
                "kgts,skd->kgtd",
                weights.astype(jnp.bfloat16),
                val_block,
                preferred_element_type=jnp.float32,
            )
            return (new_max, running_sum, accumulated)

        carried = lax.cond(jnp.any(allowed), absorb, lambda unchanged: unchanged, carried)
    running_max, running_sum, accumulated = carried
    teacher_rows = (accumulated / running_sum[..., None]).astype(jnp.bfloat16)
    teacher_rows = jnp.transpose(teacher_rows, (2, 0, 1, 3)).reshape(
        tokens, groups, t_local * HEAD_WIDTH
    )
    teacher_out = lax.all_to_all(
        teacher_rows, "seq", split_axis=1, concat_axis=0, tiled=True
    ).reshape(length, t_local * HEAD_WIDTH)
    s_heads_all = s_query.shape[2] // HEAD_WIDTH
    s_local = s_heads_all // groups
    s_kv = s_key.shape[2] // HEAD_WIDTH
    student_rows = s_query[0].reshape(tokens, groups, s_local * HEAD_WIDTH)
    student_heads = lax.all_to_all(student_rows, "seq", split_axis=1, concat_axis=0, tiled=True)
    all_keys, all_values = (
        lax.all_gather(s_key[0], "seq", axis=0, tiled=True),
        lax.all_gather(student_value[0], "seq", axis=0, tiled=True),
    )
    kv_index = my_index // (groups // s_kv)
    key_heads = lax.dynamic_slice_in_dim(all_keys, kv_index * HEAD_WIDTH, HEAD_WIDTH, 1)
    val_heads = lax.dynamic_slice_in_dim(all_values, kv_index * HEAD_WIDTH, HEAD_WIDTH, 1)
    prob_blocks, student_blocks = head_attention(
        student_heads, key_heads, val_heads, positions, stored_docs
    )
    student_out = student_blocks.reshape(length, s_local * HEAD_WIDTH)
    width_all = student_wo.shape[1]
    own_diff = lax.psum_scatter(
        (
            jnp.dot(student_out, student_wo, preferred_element_type=jnp.float32)
            - jnp.dot(teacher_out, projection, preferred_element_type=jnp.float32)
        ).astype(jnp.bfloat16),
        "seq",
        scatter_dimension=0,
        tiled=True,
    ).astype(jnp.float32)
    squares = lax.psum(jnp.sum(own_diff * own_diff), "seq")
    seq_loss = (squares / (length * width_all)).reshape(1)
    own_grad = own_diff.astype(jnp.bfloat16)
    piece_rows = lax.all_gather(own_grad, "seq", axis=0, tiled=True)
    attn_rows = jnp.einsum("rc,hc->rh", piece_rows, student_wo, preferred_element_type=jnp.float32)
    d_attn = attn_rows
    d_weight = jnp.einsum("rh,rc->hc", student_out, piece_rows, preferred_element_type=jnp.float32)
    d_attn, d_weight = (d_attn, d_weight)
    row_block = math.gcd(length, 512)
    blocks = length // row_block
    grad_blocks = d_attn.astype(jnp.bfloat16).reshape(blocks, row_block, s_local, HEAD_WIDTH)
    query_blocks = student_heads.reshape(blocks, row_block, s_local, HEAD_WIDTH)

    def back_block(carried, inputs):
        d_key, d_value = carried
        prob_block, out_block, grad_block, query_block = inputs
        row_delta = jnp.sum(grad_block.astype(jnp.float32) * out_block.astype(jnp.float32), axis=2)
        d_value = d_value + jnp.einsum(
            "hqk,qhd->kd", prob_block, grad_block, preferred_element_type=jnp.float32
        )
        d_prob = jnp.einsum(
            "qhd,kd->hqk", grad_block, val_heads, preferred_element_type=jnp.float32
        )
        d_score = (
            prob_block.astype(jnp.float32) * (d_prob - jnp.transpose(row_delta)[:, :, None])
        ).astype(jnp.bfloat16)
        d_query = (
            jnp.einsum("hqk,kd->qhd", d_score, key_heads, preferred_element_type=jnp.float32)
            * scaling
        ).astype(jnp.bfloat16)
        d_key = d_key + jnp.einsum(
            "hqk,qhd->kd", d_score, query_block, preferred_element_type=jnp.float32
        )
        return ((d_key, d_value), d_query)

    zero_rows = jnp.zeros((length, HEAD_WIDTH), jnp.float32)
    (d_key, d_value), d_query = lax.scan(
        back_block, (zero_rows, zero_rows), (prob_blocks, student_blocks, grad_blocks, query_blocks)
    )
    query_part = d_query.reshape(length, 1, s_local * HEAD_WIDTH)
    key_part = (d_key * scaling).astype(jnp.bfloat16).reshape(length, 1, HEAD_WIDTH)
    value_part = d_value.astype(jnp.bfloat16).reshape(length, 1, HEAD_WIDTH)
    back_query, back_key, back_value = (
        lax.all_to_all(query_part, "seq", split_axis=0, concat_axis=1, tiled=True),
        lax.all_to_all(key_part, "seq", split_axis=0, concat_axis=1, tiled=True),
        lax.all_to_all(value_part, "seq", split_axis=0, concat_axis=1, tiled=True),
    )
    repeat_count = groups // s_kv

    def merge_slots(slot_rows):
        summed = (
            slot_rows.reshape(tokens, s_kv, repeat_count, HEAD_WIDTH)
            .astype(jnp.float32)
            .sum(axis=2)
        )
        return summed.astype(jnp.bfloat16).reshape(1, tokens, s_kv * HEAD_WIDTH)

    weight_share = lax.psum_scatter(
        d_weight.astype(jnp.bfloat16), "rep", scatter_dimension=1, tiled=True
    ).astype(jnp.float32)
    return (
        seq_loss,
        weight_share,
        back_query.reshape(1, tokens, s_heads_all * HEAD_WIDTH),
        merge_slots(back_key),
        merge_slots(back_value),
    )


def solution(mesh):
    in_specs = (
        P("rep", "seq", None),
        P("rep", "seq", None),
        P("rep", "seq", None),
        P("rep", "seq", None),
        P("rep", "seq", None),
        P("rep", "seq", None),
        P("seq", None),
        P("seq", None),
        P("rep", None),
        P("rep", None),
    )
    out_specs = (
        P("rep"),
        P("seq", "rep"),
        P("rep", "seq", None),
        P("rep", "seq", None),
        P("rep", "seq", None),
    )
    return jax.shard_map(shards, mesh=mesh, in_specs=in_specs, out_specs=out_specs, check_vma=False)
```

profile of v0, /device:TPU:4, one launch (start us, length us, event | category | flops | bytes accessed | tf_op | source)
XLA Modules:
  0.0 964.9 jit_solution(540645325133309990)
XLA Ops:
  14.1 11.4 %all-to-all-start = ((bf16[128,16,128]{0,2,1:T(8,128)(2,1)}), bf16[128,16,128]{0,2,1:T(8,128)(2,1)S(1)}, u32[]{:S(2)}, u32[]{:S(2)}) async-start(bf16[128,16,128]{0,2,1:T(8,128)(2,1)} %bitcast.19), calls=%async_computation | async-start | bytes 1048576 | tf_op jit(solution)/shard_map/all_to_all | solution.py:124
  26.5 11.8 %gather_fusion = s32[2048]{0:T(1024)S(1)} fusion(s32[2048]{0:T(1024)S(1)} %bitcast.316, s32[2048]{0:T(1024)S(1)} %broadcast_clamp_fusion), kind=kCustom, calls=%fused_computation | custom fusion | bytes 24576 | tf_op jit(solution)/shard_map/jit(_take)/gather | solution.py:64
  45.3 55.4 %all-gather.16.cloned.1.call-done = bf16[1,2048,512]{1,2,0:T(8,128)(2,1)} async-done(((bf16[1,128,512]{1,2,0:T(8,128)(2,1)}), bf16[1,2048,512]{1,2,0:T(8,128)(2,1)}) %all-gather.16.cloned.1.call-update) | async-done | bytes 2097168 | tf_op jit(solution)/shard_map/all_gather | solution.py:79
  101.9 83.1 %all-gather.18.cloned.1.call-done = bf16[1,2048,512]{1,2,0:T(8,128)(2,1)} async-done(((bf16[1,128,512]{1,2,0:T(8,128)(2,1)}), bf16[1,2048,512]{1,2,0:T(8,128)(2,1)}) %all-gather.18.cloned.1.call-update) | async-done | bytes 2097168 | tf_op jit(solution)/shard_map/all_gather | solution.py:80
  187.1 10.2 %conditional.4 = (f32[4,8,128]{2,1,0:T(8,128)}, f32[4,8,128]{2,1,0:T(8,128)S(1)}, f32[4,8,128,128]{3,2,1,0:T(8,128)}) conditional(s32[]{:T(128)} %convert_element_type.124, () %tuple.44, (pred[128,512]{0,1:T(8,128)(4,1)S(1)}, bf16[512,4,128]{0,2,1:T(8,128)(2,1)S(1)}, bf16[128,4,8,128]{0,3,2,1:T(8,128)(2,1)S(1)}, ...), branch_computations={%region_8.9_spmd, %region_9.0_spmd} | conditional | flops 1101545472 | bytes 29736984 | solution.py:111
  197.3 11.0 %conditional.5 = ((f32[4,8,128]{2,1,0:T(8,128)}, f32[4,8,128]{2,1,0:T(8,128)S(1)}, f32[4,8,128,128]{3,2,1,0:T(8,128)})) conditional(s32[]{:T(128)} %convert_element_type.123, (f32[4,8,128]{2,1,0:T(8,128)}, f32[4,8,128]{2,1,0:T(8,128)S(1)}, f32[4,8,128,128]{3,2,1,0:T(8,128)}) %conditional.4, (pred[128,512]{0,1:T(8,128)(4,1)S(1)}, ...), branch_computations={%region_12.13_spmd, %region_13.16_spmd} | conditional | flops 1102061568 | bytes 34013244 | solution.py:111
  202.4 5.3 multiply_add_fusion
  208.3 13.6 %conditional.6 = ((f32[4,8,128]{2,1,0:T(8,128)}, f32[4,8,128]{2,1,0:T(8,128)S(1)}, f32[4,8,128,128]{3,2,1,0:T(8,128)})) conditional(s32[]{:T(128)} %convert_element_type.122, (f32[4,8,128]{2,1,0:T(8,128)}, f32[4,8,128]{2,1,0:T(8,128)S(1)}, f32[4,8,128,128]{3,2,1,0:T(8,128)}) %get-tuple-element.785, (pred[128,512]{0,1:T(8,128)(4,1)S(1)}, ...), branch_computations={%region_16.17_spmd, %region_17.20_spmd} | conditional | flops 1102061568 | bytes 34013216 | solution.py:111
  221.8 14.4 %conditional.7 = (f32[4,8,128]{2,1,0:T(8,128)S(1)}, f32[4,8,128,128]{2,3,1,0:T(8,128)S(1)}) conditional(s32[]{:T(128)} %convert_element_type.121, (f32[4,8,128]{2,1,0:T(8,128)S(1)}, f32[4,8,128,128]{3,2,1,0:T(8,128)}) %tuple.48, (pred[128,512]{0,1:T(8,128)(4,1)S(1)}, bf16[2048,512]{0,1:T(8,128)(2,1)}, bf16[128,4,8,128]{0,3,2,1:T(8,128)(2,1)S(1)}, ...), branch_computations={%region_20.21_spmd, %region_21.24_spmd} | conditional | flops 1102061568 | bytes 38174736 | solution.py:111
  237.6 7.3 all-to-all-start.1
  245.0 35.6 %all-gather.14.cloned.1.call-done = bf16[1,2048,512]{2,1,0:T(8,128)(2,1)} async-done(((bf16[1,128,512]{2,1,0:T(8,128)(2,1)}), bf16[1,2048,512]{2,1,0:T(8,128)(2,1)}) %all-gather.14.cloned.1.call-update) | async-done | bytes 2097168 | tf_op jit(solution)/shard_map/all_gather | solution.py:127
  282.6 82.9 %all-gather.12.cloned.1.call-done = bf16[1,2048,512]{2,1,0:T(8,128)(2,1)} async-done(((bf16[1,128,512]{2,1,0:T(8,128)(2,1)}), bf16[1,2048,512]{2,1,0:T(8,128)(2,1)}) %all-gather.12.cloned.1.call-update) | async-done | bytes 2097168 | tf_op jit(solution)/shard_map/all_gather | solution.py:126
  368.2 48.5 %while.28 = (s32[]{:T(128)}, bf16[4,1,512,2048]{3,2,1,0:T(8,128)(2,1)}, bf16[4,512,1,128]{3,1,2,0:T(8,128)(2,1)}, s32[4]{0:T(128)S(1)}, s32[2048]{0:T(1024)S(1)}...) while((s32[]{:T(128)}, ...), condition=%wide.region_3.4_spmd.clone, body=%wide.region_0.3_spmd.clone.sunk | while | flops 570491904 | bytes 20315468 | solution.py:43
  416.7 9.1 fusion.98
  426.3 11.3 %subtract_convert_fusion = bf16[2048,2048]{1,0:T(8,128)(2,1)} fusion(f32[2048,2048]{1,0:T(8,128)} %fusion.98, bf16[2048,256]{1,0:T(8,128)(2,1)S(1)} %bitcast.323, bf16[256,2048]{1,0:T(8,128)(2,1)S(1)} %copy-done), kind=kOutput, calls=%fused_computation.101 | convolution fusion | flops 2155872256 | bytes 27262976 | tf_op jit(solution)/shard_map/dot_general | solution.py:140
  437.9 221.5 %reduce-scatter.5.cloned.1.call-done = bf16[128,2048]{1,0:T(8,128)(2,1)} async-done(((bf16[2048,2048]{1,0:T(8,128)(2,1)}), bf16[128,2048]{1,0:T(8,128)(2,1)}) %reduce-scatter.5.cloned.1.call-update) | async-done | bytes 524304 | tf_op jit(solution)/shard_map/reduce_scatter | solution.py:137
  659.5 135.7 %all-gather.10.cloned.1.call-done = bf16[2048,2048]{1,0:T(8,128)(2,1)} async-done(((bf16[128,2048]{1,0:T(8,128)(2,1)}), bf16[2048,2048]{1,0:T(8,128)(2,1)}) %all-gather.10.cloned.1.call-update) | async-done | bytes 8388624 | tf_op jit(solution)/shard_map/all_gather | solution.py:149
  795.2 6.5 convolution_convert_fusion
  802.6 46.5 %while.29 = (s32[]{:T(128)}, f32[2048,128]{1,0:T(8,128)}, f32[2048,128]{1,0:T(8,128)}, bf16[4,512,1,128]{3,1,2,0:T(8,128)(2,1)}, bf16[4,1,512,2048]{3,2,1,0:T(8,...) while((s32[]{:T(128)}, f32[2048,128]{1,0:T(8,128)}, ...), condition=%wide.region_30.31_spmd.clone, body=%wide.region_28.30_spmd.clone.sunk | while | flops 1079377408 | bytes 18619552 | solution.py:182
  853.4 7.3 all-to-all-start.4
  862.7 11.7 %all-to-all-done.4 = bf16[16,2,8192]{2,1,0:T(2,128)(2,1)S(1)} async-done(((bf16[16,2,8192]{2,1,0:T(2,128)(2,1)}), bf16[16,2,8192]{2,1,0:T(2,128)(2,1)S(1)}, u32[]{:S(2)}, u32[]{:S(2)}) %all-to-all-start.4) | async-done | bytes 524320 | tf_op jit(solution)/shard_map/all_to_all | solution.py:191
  874.4 7.4 all-to-all-start.3
  895.1 7.2 all-to-all-start.2
  903.1 43.3 %psum.7 = f32[]{:T(128)} all-reduce(f32[]{:T(128)} %multiply_reduce_fusion.1), channel_id=1, replica_groups=mesh['seq'=16,'rep'=16] {'seq'}, use_global_device_ids=true, to_apply=%region_26.27 | all-reduce | flops 1 | bytes 8 | tf_op jit(solution)/shard_map/psum | solution.py:146
  (181 shorter events, 188.9 us)
Async XLA Ops:
  7.2 419.1 %copy-start = (bf16[256,2048]{1,0:T(8,128)(2,1)S(1)}, bf16[256,2048]{1,0:T(8,128)(2,1)}, u32[]{:S(2)}) copy-start(bf16[256,2048]{1,0:T(8,128)(2,1)} %param.29) | copy-start | bytes 3145732
  7.2 19.3 %copy-start.1 = (s32[1,2048]{1,0:T(1,128)S(1)}, s32[1,2048]{1,0:T(1,128)}, u32[]{:S(2)}) copy-start(s32[1,2048]{1,0:T(1,128)} %param.30) | copy-start | bytes 24580
  7.2 93.5 %all-gather.16.cloned.1.call-start = ((), (), s32[]{:S(2)}) async-start(), calls=%async_computation.11 | async-start | bytes 2228224 | tf_op jit(solution)/shard_map/all_gather | solution.py:79
  9.0 176.1 %all-gather.18.cloned.1.call-start = ((), (), s32[]{:S(2)}) async-start(), calls=%async_computation.12 | async-start | bytes 2228224 | tf_op jit(solution)/shard_map/all_gather | solution.py:80
  10.7 269.9 %all-gather.14.cloned.1.call-start = ((), (), s32[]{:S(2)}) async-start(), calls=%async_computation.10 | async-start | bytes 2228224 | tf_op jit(solution)/shard_map/all_gather | solution.py:127
  11.5 354.0 %all-gather.12.cloned.1.call-start = ((), (), s32[]{:S(2)}) async-start(), calls=%async_computation.9 | async-start | bytes 2228224 | tf_op jit(solution)/shard_map/all_gather | solution.py:126
  14.1 30.2 %all-to-all-start = ((bf16[128,16,128]{0,2,1:T(8,128)(2,1)}), bf16[128,16,128]{0,2,1:T(8,128)(2,1)S(1)}, u32[]{:S(2)}, u32[]{:S(2)}) async-start(bf16[128,16,128]{0,2,1:T(8,128)(2,1)} %bitcast.19), calls=%async_computation | async-start | bytes 1048576 | tf_op jit(solution)/shard_map/all_to_all | solution.py:124
  199.5 2.9 copy-start.6
  237.6 188.2 %all-to-all-start.1 = ((bf16[128,16,256]{0,2,1:T(8,128)(2,1)}), bf16[128,16,256]{0,2,1:T(8,128)(2,1)S(1)}, u32[]{:S(2)}, u32[]{:S(2)}) async-start(bf16[128,16,256]{0,2,1:T(8,128)(2,1)} %bitcast.321), calls=%async_computation.1 | async-start | bytes 2097152 | tf_op jit(solution)/shard_map/all_to_all | solution.py:117
  244.8 414.6 %reduce-scatter.5.cloned.1.call-start = ((), (), s32[]{:S(2)}) async-start(), calls=%async_computation.7 | async-start | bytes 8912896 | tf_op jit(solution)/shard_map/reduce_scatter | solution.py:137
  368.2 48.5 %copy-start.3 = (bf16[128,2048]{1,0:T(8,128)(2,1)S(1)}, bf16[128,2048]{1,0:T(8,128)(2,1)}, u32[]{:S(2)}) copy-start(bf16[128,2048]{1,0:T(8,128)(2,1)} %param.28) | copy-start | bytes 1572868
  437.6 357.6 %copy-start.4 = (bf16[128,2048]{1,0:T(8,128)(2,1)S(1)}, bf16[128,2048]{1,0:T(8,128)(2,1)}, u32[]{:S(2)}) copy-start(bf16[128,2048]{1,0:T(8,128)(2,1)} %param.28) | copy-start | bytes 1572868
  437.7 357.6 %all-gather.10.cloned.1.call-start = ((), (), s32[]{:S(2)}) async-start(), calls=%async_computation.8 | async-start | bytes 8912896 | tf_op jit(solution)/shard_map/all_gather | solution.py:149
  806.3 2.8 copy-start.5
  817.4 3.2 copy-start.5
  829.2 3.2 copy-start.5
  841.0 3.2 copy-start.5
  853.4 21.0 %all-to-all-start.4 = ((bf16[16,2,8192]{2,1,0:T(2,128)(2,1)}), bf16[16,2,8192]{2,1,0:T(2,128)(2,1)S(1)}, u32[]{:S(2)}, u32[]{:S(2)}) async-start(bf16[16,2,8192]{2,1,0:T(2,128)(2,1)} %reshape.415), calls=%async_computation.5 | async-start | bytes 1048576 | tf_op jit(solution)/shard_map/all_to_all | solution.py:191
  874.4 20.7 %all-to-all-start.3 = ((bf16[16,2,8192]{2,1,0:T(2,128)(2,1)}), bf16[16,2,8192]{2,1,0:T(2,128)(2,1)S(1)}, u32[]{:S(2)}, u32[]{:S(2)}) async-start(bf16[16,2,8192]{2,1,0:T(2,128)(2,1)} %reshape.413), calls=%async_computation.4 | async-start | bytes 1048576 | tf_op jit(solution)/shard_map/all_to_all | solution.py:190
  881.8 73.4 %reduce-scatter.7.cloned.1.call-start = ((), (), s32[]{:S(2)}) async-start(), calls=%async_computation.13 | async-start | bytes 557056
  886.7 15.6 %copy-start.2 = (bf16[128,2048]{1,0:T(8,128)(2,1)S(1)}, bf16[128,2048]{1,0:T(8,128)(2,1)}, u32[]{:S(2)}) copy-start(bf16[128,2048]{1,0:T(8,128)(2,1)} %reduce-scatter.5.cloned.1.call-done) | copy-start | bytes 1572868
  895.1 55.2 %all-to-all-start.2 = ((bf16[16,2,8192]{2,1,0:T(2,128)(2,1)}), bf16[16,2,8192]{2,1,0:T(2,128)(2,1)}, u32[]{:S(2)}, u32[]{:S(2)}) async-start(bf16[16,2,8192]{2,1,0:T(2,128)(2,1)} %reshape.411), calls=%async_computation.3 | async-start | bytes 1048576 | tf_op jit(solution)/shard_map/all_to_all | solution.py:189
Sparse Core Ops, SparseCore 0:
  11.0 89.5 all-gather.15
  103.7 81.3 all-gather.17
  187.7 92.9 all-gather.13
  283.1 82.2 all-gather.11
  437.8 221.6 reduce-scatter.4
  661.9 133.2 all-gather.9
  887.8 67.2 reduce-scatter.6
where the time goes:
time: 975 us; the launch traced here: 965 us
  waiting for transfers between devices  633 us (65%)
  matrix products  124 us (13%)
  local copies, waits for them, and re-layouts  52.3 us (5%)
  other arithmetic  49 us (5%)
  blocking collectives  43.3 us (4%)
  starting transfers between devices  41.3 us (4%)
  between operations  18.9 us (2%)
    reduce_scatter x1, waiting for transfers between devices, shards(): lax.psum_scatter((jnp.dot(student_out, student_wo, preferred_element_type...  222 us
    all_gather x1, waiting for transfers between devices, shards(): piece_rows = lax.all_gather(own_grad, 'seq', axis=0, tiled=True)  136 us
    all_gather x1, waiting for transfers between devices, shards(): val_piece = lax.all_gather(t_value[0], 'seq', axis=0, tiled=True)  83.1 us
    all_gather x1, waiting for transfers between devices, shards(): lax.all_gather(s_key[0], 'seq', axis=0, tiled=True)  82.9 us
    all_gather x1, waiting for transfers between devices, shards(): key_piece = lax.all_gather(t_key[0], 'seq', axis=0, tiled=True)  55.4 us
    psum x1, blocking collectives, shards(): squares = lax.psum(jnp.sum(own_diff * own_diff), 'seq')  43.3 us
    all_gather x1, waiting for transfers between devices, shards(): lax.all_gather(student_value[0], 'seq', axis=0, tiled=True)  35.6 us
    dot_general x4, matrix products, absorb(): jnp.einsum('kgts,skd->kgtd', weights.astype(jnp.bfloat16), val_block, pre...  20.4 us
  transfers between devices with their start and end apart: 12, of which 9 were waited for; matrix products, arithmetic and copies ran while one was open for 16% of the time, Pallas kernels for 0%

commit v1 on v0

--- a/solution.py
+++ b/solution.py
@@ -146,7 +146,8 @@
     squares = lax.psum(jnp.sum(own_diff * own_diff), "seq")
     seq_loss = (squares / (length * width_all)).reshape(1)
     own_grad = own_diff.astype(jnp.bfloat16)
-    piece_rows = lax.all_gather(own_grad, "seq", axis=0, tiled=True)
+    stack = jnp.stack([own_grad] * lax.axis_size("seq"))
+    piece_rows = jnp.concatenate(lax.all_to_all(stack, "seq", 0, 0), axis=0)
     attn_rows = jnp.einsum("rc,hc->rh", piece_rows, student_wo, preferred_element_type=jnp.float32)
     d_attn = attn_rows
     d_weight = jnp.einsum("rh,rc->hc", student_out, piece_rows, preferred_element_type=jnp.float32)

time: 975 us -> 1040 us (1.067)
  waiting for transfers between devices: 633 us -> 676 us
  starting transfers between devices: 41.3 us -> 56.8 us
    all_to_all x0 -> x1, waiting for transfers between devices: none -> 179 us  [shards(): piece_rows = jnp.concatenate(lax.all_to_all(stack, 'seq', 0, 0), axis=0)]
    all_gather x1 -> x0, waiting for transfers between devices: 136 us -> none  [shards(): piece_rows = lax.all_gather(own_grad, 'seq', axis=0, tiled=True)]
  transfers between devices with their start and end apart: 12 -> 12, of which waited for: 9 -> 9; matrix products, arithmetic and copies ran while one was open for 16% -> 15% of each run, Pallas kernels for 0% -> 0%
where the time goes in v1:
time: 1040 us; the launch traced here: 1030 us
  waiting for transfers between devices  676 us (65%)
  matrix products  124 us (12%)
  local copies, waits for them, and re-layouts  57.6 us (6%)
  starting transfers between devices  56.8 us (5%)
  other arithmetic  49 us (5%)
  blocking collectives  43.3 us (4%)
  between operations  18.9 us (2%)
    reduce_scatter x1, waiting for transfers between devices, shards(): lax.psum_scatter((jnp.dot(student_out, student_wo, preferred_element_type...  222 us
    all_to_all x1, waiting for transfers between devices, shards(): piece_rows = jnp.concatenate(lax.all_to_all(stack, 'seq', 0, 0), axis=0)  179 us
    all_gather x1, waiting for transfers between devices, shards(): val_piece = lax.all_gather(t_value[0], 'seq', axis=0, tiled=True)  83.1 us
    all_gather x1, waiting for transfers between devices, shards(): lax.all_gather(s_key[0], 'seq', axis=0, tiled=True)  82.9 us
    all_gather x1, waiting for transfers between devices, shards(): key_piece = lax.all_gather(t_key[0], 'seq', axis=0, tiled=True)  55.4 us
    psum x1, blocking collectives, shards(): squares = lax.psum(jnp.sum(own_diff * own_diff), 'seq')  43.3 us
    all_gather x1, waiting for transfers between devices, shards(): lax.all_gather(student_value[0], 'seq', axis=0, tiled=True)  35.6 us
  transfers between devices with their start and end apart: 12, of which 9 were waited for; matrix products, arithmetic and copies ran while one was open for 15% of the time, Pallas kernels for 0%

profile of v1, /device:TPU:4, one launch (start us, length us, event | category | flops | bytes accessed | tf_op | source)
XLA Modules:
  0.0 1029.0 jit_solution(13041745403591065549)
XLA Ops:
  14.1 11.4 %all-to-all-start = ((bf16[128,16,128]{0,2,1:T(8,128)(2,1)}), bf16[128,16,128]{0,2,1:T(8,128)(2,1)S(1)}, u32[]{:S(2)}, u32[]{:S(2)}) async-start(bf16[128,16,128]{0,2,1:T(8,128)(2,1)} %bitcast.19), calls=%async_computation | async-start | bytes 1048576 | tf_op jit(solution)/shard_map/all_to_all | solution.py:124
  26.5 11.8 %gather_fusion = s32[2048]{0:T(1024)S(1)} fusion(s32[2048]{0:T(1024)S(1)} %bitcast.317, s32[2048]{0:T(1024)S(1)} %broadcast_clamp_fusion), kind=kCustom, calls=%fused_computation | custom fusion | bytes 24576 | tf_op jit(solution)/shard_map/jit(_take)/gather | solution.py:64
  45.3 55.4 %all-gather.13.cloned.1.call-done = bf16[1,2048,512]{1,2,0:T(8,128)(2,1)} async-done(((bf16[1,128,512]{1,2,0:T(8,128)(2,1)}), bf16[1,2048,512]{1,2,0:T(8,128)(2,1)}) %all-gather.13.cloned.1.call-update) | async-done | bytes 2097168 | tf_op jit(solution)/shard_map/all_gather | solution.py:79
  101.9 83.1 %all-gather.15.cloned.1.call-done = bf16[1,2048,512]{1,2,0:T(8,128)(2,1)} async-done(((bf16[1,128,512]{1,2,0:T(8,128)(2,1)}), bf16[1,2048,512]{1,2,0:T(8,128)(2,1)}) %all-gather.15.cloned.1.call-update) | async-done | bytes 2097168 | tf_op jit(solution)/shard_map/all_gather | solution.py:80
  187.1 10.2 conditional.4
  197.3 11.0 %conditional.5 = ((f32[4,8,128]{2,1,0:T(8,128)}, f32[4,8,128]{2,1,0:T(8,128)S(1)}, f32[4,8,128,128]{3,2,1,0:T(8,128)})) conditional(s32[]{:T(128)} %convert_element_type.123, (f32[4,8,128]{2,1,0:T(8,128)}, f32[4,8,128]{2,1,0:T(8,128)S(1)}, f32[4,8,128,128]{3,2,1,0:T(8,128)}) %conditional.4, (pred[128,512]{0,1:T(8,128)(4,1)S(1)}, ...), branch_computations={%region_12.13_spmd, %region_13.16_spmd} | conditional | flops 1102061568 | bytes 34013244 | solution.py:111
  208.3 13.6 %conditional.6 = ((f32[4,8,128]{2,1,0:T(8,128)}, f32[4,8,128]{2,1,0:T(8,128)S(1)}, f32[4,8,128,128]{3,2,1,0:T(8,128)})) conditional(s32[]{:T(128)} %convert_element_type.122, (f32[4,8,128]{2,1,0:T(8,128)}, f32[4,8,128]{2,1,0:T(8,128)S(1)}, f32[4,8,128,128]{3,2,1,0:T(8,128)}) %get-tuple-element.785, (pred[128,512]{0,1:T(8,128)(4,1)S(1)}, ...), branch_computations={%region_16.17_spmd, %region_17.20_spmd} | conditional | flops 1102061568 | bytes 34013216 | solution.py:111
  221.8 14.4 %conditional.7 = (f32[4,8,128]{2,1,0:T(8,128)S(1)}, f32[4,8,128,128]{2,3,1,0:T(8,128)S(1)}) conditional(s32[]{:T(128)} %convert_element_type.121, (f32[4,8,128]{2,1,0:T(8,128)S(1)}, f32[4,8,128,128]{3,2,1,0:T(8,128)}) %tuple.48, (pred[128,512]{0,1:T(8,128)(4,1)S(1)}, bf16[2048,512]{0,1:T(8,128)(2,1)}, bf16[128,4,8,128]{0,3,2,1:T(8,128)(2,1)S(1)}, ...), branch_computations={%region_20.21_spmd, %region_21.24_spmd} | conditional | flops 1102061568 | bytes 38174736 | solution.py:111
  237.6 7.3 all-to-all-start.1
  245.0 35.6 %all-gather.11.cloned.1.call-done = bf16[1,2048,512]{2,1,0:T(8,128)(2,1)} async-done(((bf16[1,128,512]{2,1,0:T(8,128)(2,1)}), bf16[1,2048,512]{2,1,0:T(8,128)(2,1)}) %all-gather.11.cloned.1.call-update) | async-done | bytes 2097168 | tf_op jit(solution)/shard_map/all_gather | solution.py:127
  282.6 82.9 %all-gather.9.cloned.1.call-done = bf16[1,2048,512]{2,1,0:T(8,128)(2,1)} async-done(((bf16[1,128,512]{2,1,0:T(8,128)(2,1)}), bf16[1,2048,512]{2,1,0:T(8,128)(2,1)}) %all-gather.9.cloned.1.call-update) | async-done | bytes 2097168 | tf_op jit(solution)/shard_map/all_gather | solution.py:126
  368.2 48.5 %while.28 = (s32[]{:T(128)}, bf16[4,1,512,2048]{3,2,1,0:T(8,128)(2,1)}, bf16[4,512,1,128]{3,1,2,0:T(8,128)(2,1)}, s32[4]{0:T(128)S(1)}, s32[2048]{0:T(1024)S(1)}...) while((s32[]{:T(128)}, ...), condition=%wide.region_3.4_spmd.clone, body=%wide.region_0.3_spmd.clone.sunk | while | flops 570491904 | bytes 20315468 | solution.py:43
  416.7 9.1 fusion.98
  426.3 11.3 %subtract_convert_fusion = bf16[2048,2048]{1,0:T(8,128)(2,1)} fusion(f32[2048,2048]{1,0:T(8,128)} %fusion.98, bf16[2048,256]{1,0:T(8,128)(2,1)S(1)} %bitcast.324, bf16[256,2048]{1,0:T(8,128)(2,1)S(1)} %copy-done), kind=kOutput, calls=%fused_computation.101 | convolution fusion | flops 2155872256 | bytes 27262976 | tf_op jit(solution)/shard_map/dot_general | solution.py:140
  437.7 222.0 %reduce-scatter.5.cloned.1.call-done = bf16[128,2048]{1,0:T(8,128)(2,1)} async-done(((bf16[2048,2048]{1,0:T(8,128)(2,1)}), bf16[128,2048]{1,0:T(8,128)(2,1)}) %reduce-scatter.5.cloned.1.call-update) | async-done | bytes 524304 | tf_op jit(solution)/shard_map/reduce_scatter | solution.py:137
  664.9 9.3 all-to-all-start.2
  674.3 178.8 %all-to-all-done.2 = bf16[16,128,2048]{2,1,0:T(8,128)(2,1)} async-done(((bf16[16,128,2048]{2,1,0:T(8,128)(2,1)}), bf16[16,128,2048]{2,1,0:T(8,128)(2,1)}, u32[]{:S(2)}, u32[]{:S(2)}) %all-to-all-start.2) | async-done | bytes 8388640 | tf_op jit(solution)/shard_map/all_to_all | solution.py:150
  853.1 6.6 convolution_convert_fusion
  860.6 46.5 %while.29 = (s32[]{:T(128)}, f32[2048,128]{1,0:T(8,128)}, f32[2048,128]{1,0:T(8,128)}, bf16[4,512,1,128]{3,1,2,0:T(8,128)(2,1)}, bf16[4,1,512,2048]{3,2,1,0:T(8,...) while((s32[]{:T(128)}, f32[2048,128]{1,0:T(8,128)}, ...), condition=%wide.region_30.31_spmd.clone, body=%wide.region_28.30_spmd.clone.sunk | while | flops 1079377408 | bytes 18619552 | solution.py:183
  911.3 13.7 %all-to-all-start.5 = ((bf16[16,2,8192]{2,1,0:T(2,128)(2,1)}), bf16[16,2,8192]{2,1,0:T(2,128)(2,1)S(1)}, u32[]{:S(2)}, u32[]{:S(2)}) async-start(bf16[16,2,8192]{2,1,0:T(2,128)(2,1)} %reshape.421), calls=%async_computation.6 | async-start | bytes 1048576 | tf_op jit(solution)/shard_map/all_to_all | solution.py:192
  926.9 11.5 %all-to-all-done.5 = bf16[16,2,8192]{2,1,0:T(2,128)(2,1)S(1)} async-done(((bf16[16,2,8192]{2,1,0:T(2,128)(2,1)}), bf16[16,2,8192]{2,1,0:T(2,128)(2,1)S(1)}, u32[]{:S(2)}, u32[]{:S(2)}) %all-to-all-start.5) | async-done | bytes 524320 | tf_op jit(solution)/shard_map/all_to_all | solution.py:192
  938.3 7.4 all-to-all-start.4
  959.1 7.3 all-to-all-start.3
  967.2 43.3 %psum.7 = f32[]{:T(128)} all-reduce(f32[]{:T(128)} %multiply_reduce_fusion.1), channel_id=1, replica_groups=mesh['seq'=16,'rep'=16] {'seq'}, use_global_device_ids=true, to_apply=%region_26.27 | all-reduce | flops 1 | bytes 8 | tf_op jit(solution)/shard_map/psum | solution.py:146
  (181 shorter events, 199.2 us)
Async XLA Ops:
  7.2 419.1 %copy-start = (bf16[256,2048]{1,0:T(8,128)(2,1)S(1)}, bf16[256,2048]{1,0:T(8,128)(2,1)}, u32[]{:S(2)}) copy-start(bf16[256,2048]{1,0:T(8,128)(2,1)} %param.29) | copy-start | bytes 3145732
  7.2 19.3 %copy-start.1 = (s32[1,2048]{1,0:T(1,128)S(1)}, s32[1,2048]{1,0:T(1,128)}, u32[]{:S(2)}) copy-start(s32[1,2048]{1,0:T(1,128)} %param.30) | copy-start | bytes 24580
  7.2 93.5 %all-gather.13.cloned.1.call-start = ((), (), s32[]{:S(2)}) async-start(), calls=%async_computation.11 | async-start | bytes 2228224 | tf_op jit(solution)/shard_map/all_gather | solution.py:79
  9.0 176.1 %all-gather.15.cloned.1.call-start = ((), (), s32[]{:S(2)}) async-start(), calls=%async_computation.12 | async-start | bytes 2228224 | tf_op jit(solution)/shard_map/all_gather | solution.py:80
  10.7 269.9 %all-gather.11.cloned.1.call-start = ((), (), s32[]{:S(2)}) async-start(), calls=%async_computation.10 | async-start | bytes 2228224 | tf_op jit(solution)/shard_map/all_gather | solution.py:127
  11.5 354.0 %all-gather.9.cloned.1.call-start = ((), (), s32[]{:S(2)}) async-start(), calls=%async_computation.9 | async-start | bytes 2228224 | tf_op jit(solution)/shard_map/all_gather | solution.py:126
  14.1 30.2 %all-to-all-start = ((bf16[128,16,128]{0,2,1:T(8,128)(2,1)}), bf16[128,16,128]{0,2,1:T(8,128)(2,1)S(1)}, u32[]{:S(2)}, u32[]{:S(2)}) async-start(bf16[128,16,128]{0,2,1:T(8,128)(2,1)} %bitcast.19), calls=%async_computation | async-start | bytes 1048576 | tf_op jit(solution)/shard_map/all_to_all | solution.py:124
  199.5 2.9 copy-start.6
  237.6 188.2 %all-to-all-start.1 = ((bf16[128,16,256]{0,2,1:T(8,128)(2,1)}), bf16[128,16,256]{0,2,1:T(8,128)(2,1)S(1)}, u32[]{:S(2)}, u32[]{:S(2)}) async-start(bf16[128,16,256]{0,2,1:T(8,128)(2,1)} %bitcast.322), calls=%async_computation.1 | async-start | bytes 2097152 | tf_op jit(solution)/shard_map/all_to_all | solution.py:117
  244.8 414.8 %reduce-scatter.5.cloned.1.call-start = ((), (), s32[]{:S(2)}) async-start(), calls=%async_computation.8 | async-start | bytes 8912896 | tf_op jit(solution)/shard_map/reduce_scatter | solution.py:137
  368.2 48.5 %copy-start.3 = (bf16[128,2048]{1,0:T(8,128)(2,1)S(1)}, bf16[128,2048]{1,0:T(8,128)(2,1)}, u32[]{:S(2)}) copy-start(bf16[128,2048]{1,0:T(8,128)(2,1)} %param.28) | copy-start | bytes 1572868
  664.9 188.2 %copy-start.4 = (bf16[128,2048]{1,0:T(8,128)(2,1)S(1)}, bf16[128,2048]{1,0:T(8,128)(2,1)}, u32[]{:S(2)}) copy-start(bf16[128,2048]{1,0:T(8,128)(2,1)} %param.28) | copy-start | bytes 1572868
  664.9 188.2 %all-to-all-start.2 = ((bf16[16,128,2048]{2,1,0:T(8,128)(2,1)}), bf16[16,128,2048]{2,1,0:T(8,128)(2,1)}, u32[]{:S(2)}, u32[]{:S(2)}) async-start(bf16[16,128,2048]{2,1,0:T(8,128)(2,1)} %stack.2), calls=%async_computation.3 | async-start | bytes 16777216 | tf_op jit(solution)/shard_map/all_to_all | solution.py:150
  864.2 2.8 copy-start.5
  875.3 3.2 copy-start.5
  887.1 3.2 copy-start.5
  898.9 3.2 copy-start.5
  911.3 27.1 %all-to-all-start.5 = ((bf16[16,2,8192]{2,1,0:T(2,128)(2,1)}), bf16[16,2,8192]{2,1,0:T(2,128)(2,1)S(1)}, u32[]{:S(2)}, u32[]{:S(2)}) async-start(bf16[16,2,8192]{2,1,0:T(2,128)(2,1)} %reshape.421), calls=%async_computation.6 | async-start | bytes 1048576 | tf_op jit(solution)/shard_map/all_to_all | solution.py:192
  938.3 20.7 %all-to-all-start.4 = ((bf16[16,2,8192]{2,1,0:T(2,128)(2,1)}), bf16[16,2,8192]{2,1,0:T(2,128)(2,1)S(1)}, u32[]{:S(2)}, u32[]{:S(2)}) async-start(bf16[16,2,8192]{2,1,0:T(2,128)(2,1)} %reshape.419), calls=%async_computation.5 | async-start | bytes 1048576 | tf_op jit(solution)/shard_map/all_to_all | solution.py:191
  945.8 73.5 %reduce-scatter.7.cloned.1.call-start = ((), (), s32[]{:S(2)}) async-start(), calls=%async_computation.13 | async-start | bytes 557056
  950.7 15.7 %copy-start.2 = (bf16[128,2048]{1,0:T(8,128)(2,1)S(1)}, bf16[128,2048]{1,0:T(8,128)(2,1)}, u32[]{:S(2)}) copy-start(bf16[128,2048]{1,0:T(8,128)(2,1)} %reduce-scatter.5.cloned.1.call-done) | copy-start | bytes 1572868
  959.1 55.3 %all-to-all-start.3 = ((bf16[16,2,8192]{2,1,0:T(2,128)(2,1)}), bf16[16,2,8192]{2,1,0:T(2,128)(2,1)}, u32[]{:S(2)}, u32[]{:S(2)}) async-start(bf16[16,2,8192]{2,1,0:T(2,128)(2,1)} %reshape.417), calls=%async_computation.4 | async-start | bytes 1048576 | tf_op jit(solution)/shard_map/all_to_all | solution.py:190
Sparse Core Ops, SparseCore 0:
  11.0 89.5 all-gather.12
  103.7 81.3 all-gather.14
  187.7 92.9 all-gather.10
  283.1 82.2 all-gather.8
  437.8 221.8 reduce-scatter.4
  951.8 67.4 reduce-scatter.6
